TPU v7x, 32 devices: a whole 2x2x4 slice. The times are simulated.
32 devices in a mesh: dp: 8 (over z, x), mp: 4 (over y, core).
Axes of the slice: x: 2, y: 2, z: 4, core: 2. Of those that a mesh axis runs over, the one named last changes fastest.
Arguments:
- features: bfloat16 [8192, 1024], P('dp'), may hold values from -6 to 6
- out_grads: bfloat16 [8192, 4, 1024], P('dp', None, 'mp'), may hold values from -0.0625 to 0.0625
- norm_grads: float32 [8, 2048], P('dp'), may hold values from -2 to 2
- owners: int32 [5], replicated, may hold values from 0 to 7, as said below
- moment1: float32 [4, 1024, 1024], P(None, 'dp', 'mp'), may hold values from -6 to 6
- moment2: float32 [4, 1024, 1024], P(None, 'dp', 'mp'), may hold values from 0.1 to 10
- left_stats: float32 [4, 1024, 1024], P(None, 'dp', 'mp'), may hold values from -1024 to 1024, as said below
- right_stats: float32 [4, 1024, 1024], P(None, 'dp', 'mp'), may hold values from -1024 to 1024, as said below
- left_basis: float32 [4, 1024, 1024], P(None, 'dp', 'mp'), may hold values from -1 to 2
- right_basis: float32 [4, 1024, 1024], P(None, 'dp', 'mp'), may hold values from -1 to 2
- norm_m: float32 [2048], P('dp'), may hold values from -6 to 6
- norm_v: float32 [2048], P('dp'), may hold values from 0.1 to 10
Outputs:
- new_moment1: float32 [4, 1024, 1024], P(None, 'dp', 'mp')
- new_moment2: float32 [4, 1024, 1024], P(None, 'dp', 'mp')
- new_left_stats: float32 [4, 1024, 1024], P(None, 'dp', 'mp')
- new_right_stats: float32 [4, 1024, 1024], P(None, 'dp', 'mp')
- new_left_basis: float32 [4, 1024, 1024], P(None, 'dp', 'mp')
- new_right_basis: float32 [4, 1024, 1024], P(None, 'dp', 'mp')
- update_slots: bfloat16 [8, 1024, 1024], P('dp', None, 'mp')
- new_norm_m: float32 [2048], P('dp')
- new_norm_v: float32 [2048], P('dp')
- norm_slots: float32 [8, 2048], P('dp')
Inputs may be any that keep to these rules, and one draw needn't show every extreme that they name: `owners`: the first 4 entries are distinct, so a dp index owns at most one tile; the last entry may equal any of them. `left_stats`: each tile of statistics is symmetric. `right_stats`: each tile of statistics is symmetric.
All inputs are finite; a program needn't handle non-finite values.
Results may differ from a plain program's by a relative error of at most 0.0072.
Values may be sent and summed in bfloat16 or wider, within the bound.
A program may use at most 128 MiB of HBM per device.

v0:
```python
import jax
import jax.numpy as jnp
from jax import lax
from jax.sharding import PartitionSpec as P

FIX_ONE = 1.0 - 0.9**10
FIX_TWO = 1.0 - 0.95**10
BF = jnp.bfloat16
F32 = jnp.float32


def contract(left, right, left_dim, right_dim):
    return lax.dot_general(
        left, right, (((left_dim,), (right_dim,)), ((), ())), preferred_element_type=F32
    )


def to_tile(blocks):
    out = lax.all_to_all(blocks, "mp", split_axis=1, concat_axis=1, tiled=True)
    k, n, r, c = out.shape
    return out.transpose(0, 2, 1, 3).reshape(k, r, n * c)


def to_home(rows, n):
    k, r, c = rows.shape
    out = rows.reshape(k, r, n, c // n).transpose(0, 2, 1, 3)
    return lax.all_to_all(out, "mp", split_axis=1, concat_axis=1, tiled=True)


def gather_rows(rows):
    return lax.all_gather(rows, "dp", axis=0, tiled=True)


def normalize(power):
    wide = power.astype(F32)
    return lax.rsqrt(jnp.sum(wide * wide, axis=0, keepdims=True) + 1e-06)


def shards(
    features,
    out_grads,
    norm_grads,
    owners,
    moment1,
    moment2,
    left_stats,
    right_stats,
    left_basis,
    right_basis,
    norm_m,
    norm_v,
):
    dp = lax.axis_size("dp")
    tiles, slab, width = moment1.shape
    full = slab * dp
    me = lax.axis_index("dp")
    row0 = me * slab
    narrow = to_tile(jnp.stack([left_basis, right_basis, left_stats, right_stats]).astype(BF))
    left_full = gather_rows(narrow[0])
    right_full = gather_rows(narrow[1])
    flat = out_grads.reshape(out_grads.shape[0], tiles * width)
    partial = contract(features, flat, 0, 0).astype(BF).reshape(dp, slab, tiles * width)
    parts = lax.all_to_all(partial, "dp", split_axis=0, concat_axis=0, tiled=True)
    grad_home = jnp.sum(parts.astype(F32), axis=0).astype(BF)
    grad_home = grad_home.reshape(slab, tiles, width).transpose(1, 0, 2)
    grad_rows = to_tile(grad_home[None])[0]
    grad_full = gather_rows(grad_rows)
    wide = to_tile(jnp.stack([moment1, moment2]))
    prod_l = contract(grad_rows, grad_full, 1, 1)
    grad_cols = lax.dynamic_slice_in_dim(grad_full, row0, slab, 1)
    prod_r = contract(grad_cols, grad_full, 0, 0)
    stats_l = (0.95 * narrow[2].astype(F32) + 0.05 * prod_l).astype(BF)
    stats_r = (0.95 * narrow[3].astype(F32) + 0.05 * prod_r).astype(BF)
    power_l = contract(stats_l, left_full, 1, 0).astype(BF)
    power_r = contract(stats_r, right_full, 1, 0).astype(BF)
    power_l_full = gather_rows(power_l)
    power_r_full = gather_rows(power_r)
    left_cols = lax.dynamic_slice_in_dim(left_full, row0, slab, 1)
    half = contract(left_cols, grad_full, 0, 0).astype(BF)
    rotated = contract(half, right_full, 1, 0)
    tile_one = 0.9 * wide[0] + 0.1 * rotated
    tile_two = 0.95 * wide[1] + 0.05 * rotated * rotated
    direction = (tile_one / FIX_ONE / (jnp.sqrt(tile_two / FIX_TWO) + 1e-08)).astype(BF)
    back = contract(direction, right_full, 1, 1).astype(BF)
    back_full = gather_rows(back)
    home1 = to_home(jnp.stack([rotated, prod_l, prod_r]).astype(BF), tiles).astype(F32)
    new_one = 0.9 * moment1 + 0.1 * home1[0]
    new_two = 0.95 * moment2 + 0.05 * home1[0] * home1[0]
    new_sl = 0.95 * left_stats + 0.05 * home1[1]
    new_sr = 0.95 * right_stats + 0.05 * home1[2]
    update = contract(narrow[0], back_full, 1, 0).astype(BF)

    def refine(power_full, power_rows):
        scale = normalize(power_full)
        iter_full = (power_full.astype(F32) * scale).astype(BF)
        iter_rows = (power_rows.astype(F32) * scale).astype(BF)
        gram = contract(iter_rows, iter_full, 1, 1).astype(BF)
        return 1.5 * iter_rows.astype(F32) - 0.5 * contract(gram, iter_full, 1, 0)

    new_l = refine(power_l_full, power_l)
    new_r = refine(power_r_full, power_r)
    home2 = to_home(jnp.stack([new_l.astype(BF), new_r.astype(BF), update]), tiles)
    new_bl = home2[0].astype(F32)
    new_br = home2[1].astype(F32)
    slot_of = jnp.arange(dp, dtype=jnp.int32)[:, None, None]
    slots = jnp.zeros((dp, slab, width), BF)
    for n in range(tiles):
        slots = jnp.where(slot_of == owners[n], home2[2, n][None], slots)
    update_slot = lax.all_to_all(slots, "dp", split_axis=0, concat_axis=0, tiled=True)
    update_slot = update_slot.reshape(1, full, width)
    packed = jnp.concatenate([norm_grads[0], norm_m, norm_v])[None]
    everyone = lax.all_gather(packed, "dp", axis=0, tiled=True)
    size = norm_grads.shape[1]
    part = norm_m.shape[0]
    norm_total = jnp.sum(everyone[:, :size], axis=0)
    all_nm = 0.9 * everyone[:, size : size + part].reshape(size) + 0.1 * norm_total
    all_nv = 0.95 * everyone[:, size + part :].reshape(size) + 0.05 * norm_total * norm_total
    norm_step = all_nm / FIX_ONE / (jnp.sqrt(all_nv / FIX_TWO) + 1e-08)
    norm_slot = jnp.where(me == owners[tiles], norm_step, 0.0)[None]
    new_nm = lax.dynamic_slice_in_dim(all_nm, me * part, part, 0)
    new_nv = lax.dynamic_slice_in_dim(all_nv, me * part, part, 0)
    return (
        new_one,
        new_two,
        new_sl,
        new_sr,
        new_bl,
        new_br,
        update_slot,
        new_nm,
        new_nv,
        norm_slot,
    )


def solution(mesh):
    in_specs = (
        P("dp", None),
        P("dp", None, "mp"),
        P("dp", None),
        P(),
        P(None, "dp", "mp"),
        P(None, "dp", "mp"),
        P(None, "dp", "mp"),
        P(None, "dp", "mp"),
        P(None, "dp", "mp"),
        P(None, "dp", "mp"),
        P("dp"),
        P("dp"),
    )
    out_specs = (
        P(None, "dp", "mp"),
        P(None, "dp", "mp"),
        P(None, "dp", "mp"),
        P(None, "dp", "mp"),
        P(None, "dp", "mp"),
        P(None, "dp", "mp"),
        P("dp", None, "mp"),
        P("dp"),
        P("dp"),
        P("dp", None),
    )
    return jax.shard_map(shards, mesh=mesh, in_specs=in_specs, out_specs=out_specs, check_vma=False)
```

profile of v0, /device:TPU:0, one launch (start us, length us, event | category | flops | bytes accessed | tf_op | source)
XLA Modules:
  0.0 471.3 jit_solution(4801705262632254614)
XLA Ops:
  7.2 2.2 copy.123
  9.5 2.4 convolution_convert_fusion
  11.9 55.4 %all_to_all.35 = bf16[8,128,1024]{2,1,0:T(8,128)(2,1)} all-to-all(bf16[8,128,1024]{2,1,0:T(8,128)(2,1)S(1)} %bitcast.132), channel_id=1, replica_groups=mesh['dp'=8,'mp'=4] {'dp'}, dimensions={0} | all-to-all | bytes 4194304 | tf_op jit(solution)/shard_map/all_to_all | solution.py:63
  67.3 2.0 reduce_sum.41
  70.2 1.1 copy.98
  71.3 9.1 %all_to_all.36 = bf16[1,4,128,256]{3,2,0,1:T(8,128)(2,1)} all-to-all(bf16[1,4,128,256]{3,2,0,1:T(8,128)(2,1)S(1)} %copy.98), channel_id=1, replica_groups=mesh['dp'=8,'mp'=4] {'mp'}, dimensions={1} | all-to-all | bytes 524288 | tf_op jit(solution)/shard_map/all_to_all | solution.py:19
  80.3 1.8 copy.99
  82.6 1.2 copy.93
  83.8 1.2 copy.92
  85.2 16.9 %all_to_all.37 = bf16[4,4,128,256]{2,3,0,1:T(8,128)(2,1)S(1)} all-to-all(bf16[4,4,128,256]{2,3,0,1:T(8,128)(2,1)S(1)} %pad_maximum_fusion), channel_id=1, replica_groups=mesh['dp'=8,'mp'=4] {'mp'}, dimensions={1} | all-to-all | bytes 2097152 | tf_op jit(solution)/shard_map/all_to_all | solution.py:19
  103.8 1.1 convert_multiply_fusion.5
  104.8 1.2 copy.117
  106.1 24.6 %all-gather.11.cloned.1.call-done = bf16[1024,1024]{0,1:T(8,128)(2,1)} async-done(((bf16[128,1024]{0,1:T(8,128)(2,1)}), bf16[1024,1024]{0,1:T(8,128)(2,1)}) %all-gather.11.cloned.1.call-update) | async-done | bytes 2097168 | tf_op jit(solution)/shard_map/all_gather | solution.py:31
  130.6 3.4 fusion.89
  134.0 47.8 %all-gather.13.cloned.1.call-done = bf16[1024,1024]{0,1:T(8,128)(2,1)} async-done(((bf16[128,1024]{0,1:T(8,128)(2,1)}), bf16[1024,1024]{0,1:T(8,128)(2,1)}) %all-gather.13.cloned.1.call-update) | async-done | bytes 2097168 | tf_op jit(solution)/shard_map/all_gather | solution.py:31
  181.8 3.3 convolution_convert_fusion.3
  185.5 2.8 fusion.90
  188.2 44.8 %all-gather.9.cloned.1.call-done = bf16[1024,1024]{0,1:T(8,128)(2,1)} async-done(((bf16[128,1024]{0,1:T(8,128)(2,1)}), bf16[1024,1024]{0,1:T(8,128)(2,1)}) %all-gather.9.cloned.1.call-update) | async-done | bytes 2097168 | tf_op jit(solution)/shard_map/all_gather | solution.py:31
  233.0 3.1 convolution_convert_fusion.4
  236.2 1.2 copy.108
  237.5 1.2 copy.109
  238.8 17.0 %all_to_all.38 = f32[2,4,128,256]{2,3,0,1:T(8,128)S(1)} all-to-all(f32[2,4,128,256]{2,3,0,1:T(8,128)S(1)} %pad_maximum_fusion.1), channel_id=1, replica_groups=mesh['dp'=8,'mp'=4] {'mp'}, dimensions={1} | all-to-all | bytes 2097152 | tf_op jit(solution)/shard_map/all_to_all | solution.py:19
  257.2 4.8 %fusion.91 = (bf16[128,1024]{1,0:T(8,128)(2,1)}, f32[128,1024]{1,0:T(8,128)}) fusion(bf16[1024,1024]{0,1:T(8,128)(2,1)} %all-gather.13.cloned.1.call-done, bf16[1024,1024]{0,1:T(8,128)(2,1)} %all-gather.11.cloned.1.call-done, bf16[1024,1024]{0,1:T(8,128)(2,1)} %all-gather.9.cloned.1.call-done, s32[]{:T(128)S(6)} %select_n.36), kind=kOutput, calls=%fused_computation.119 | convolution fusion | flops 537133056 | bytes 5242884 | tf_op jit(solution)/shard_map/dot_general | solution.py:13
  261.9 3.1 convolution_convert_fusion.2
  265.8 17.1 %all-gather.17.cloned.1.call-done = bf16[1024,1024]{1,0:T(8,128)(2,1)} async-done(((bf16[128,1024]{1,0:T(8,128)(2,1)}), bf16[1024,1024]{1,0:T(8,128)(2,1)}) %all-gather.17.cloned.1.call-update) | async-done | bytes 2097168 | tf_op jit(solution)/shard_map/all_gather | solution.py:31
  282.9 2.1 fusion.2
  285.0 3.5 fusion.24
  288.7 43.9 %all-gather.15.cloned.1.call-done = bf16[1024,1024]{1,0:T(8,128)(2,1)} async-done(((bf16[128,1024]{1,0:T(8,128)(2,1)}), bf16[1024,1024]{1,0:T(8,128)(2,1)}) %all-gather.15.cloned.1.call-update) | async-done | bytes 2097168 | tf_op jit(solution)/shard_map/all_gather | solution.py:31
  332.5 2.1 fusion
  334.6 3.5 fusion.27
  338.4 44.4 %all-gather.19.cloned.1.call-done = bf16[1024,1024]{1,0:T(8,128)(2,1)} async-done(((bf16[128,1024]{1,0:T(8,128)(2,1)}), bf16[1024,1024]{1,0:T(8,128)(2,1)}) %all-gather.19.cloned.1.call-update) | async-done | bytes 2097168 | tf_op jit(solution)/shard_map/all_gather | solution.py:31
  382.7 2.1 convolution_convert_fusion.1
  386.0 3.6 all-to-all-start.5
  389.7 30.5 %all-gather.1 = f32[8,1,2560]{2,1,0:T(1,128)S(1)} all-gather(f32[1,1,2560]{2,1,0:T(1,128)S(1)} %reshape.191), channel_id=2, replica_groups=mesh['dp'=8,'mp'=4] {'dp'}, dimensions={0}, use_global_device_ids=true | all-gather | bytes 92160 | tf_op jit(solution)/shard_map/all_gather | solution.py:112
  420.2 1.3 iota_compare_fusion
  421.6 1.8 stack.58
  423.4 1.7 copy.100
  426.0 1.7 copy.102
  427.9 2.0 maximum_bitcast_fusion
  429.9 4.2 all-to-all-start.3
  434.1 1.3 iota_compare_fusion.2
  436.7 1.1 select_select_fusion
  437.8 8.0 %all-to-all-done.3 = bf16[3,4,128,256]{3,2,0,1:T(8,128)(2,1)} async-done(((bf16[3,4,128,256]{3,2,0,1:T(8,128)(2,1)}), bf16[3,4,128,256]{3,2,0,1:T(8,128)(2,1)}, u32[]{:S(2)}, u32[]{:S(2)}) %all-to-all-start.3) | async-done | bytes 786464 | tf_op jit(solution)/shard_map/all_to_all | solution.py:27
  445.8 3.5 all-to-all-start.6
  450.0 1.3 convert_element_type.101
  451.3 1.5 fusion.48
  452.8 1.1 fusion.54
  453.8 9.8 %all-to-all-done.6 = bf16[8,128,256]{2,1,0:T(8,128)(2,1)S(1)} async-done(((bf16[8,128,256]{2,1,0:T(8,128)(2,1)}), bf16[8,128,256]{2,1,0:T(8,128)(2,1)S(1)}, u32[]{:S(2)}, u32[]{:S(2)}) %all-to-all-start.6) | async-done | bytes 524320 | tf_op jit(solution)/shard_map/all_to_all | solution.py:109
  (89 shorter events, 10.5 us)
Async XLA Ops:
  7.2 2.3 copy-start
  7.2 123.5 %all-gather.11.cloned.1.call-start = ((), (), s32[]{:S(2)}) async-start(), calls=%async_computation.8 | async-start | bytes 2359296 | tf_op jit(solution)/shard_map/all_gather | solution.py:31
  67.3 14.9 %copy-start.4 = (f32[4,128,256]{2,1,0:T(8,128)S(1)}, f32[4,128,256]{2,1,0:T(8,128)}, u32[]{:S(2)}) copy-start(f32[4,128,256]{2,1,0:T(8,128)} %param.19) | copy-start | bytes 1572868
  69.3 13.1 %copy-start.6 = (f32[4,128,256]{2,1,0:T(8,128)S(1)}, f32[4,128,256]{2,1,0:T(8,128)}, u32[]{:S(2)}) copy-start(f32[4,128,256]{2,1,0:T(8,128)} %param.18) | copy-start | bytes 1572868
  82.2 99.7 %all-gather.13.cloned.1.call-start = ((), (), s32[]{:S(2)}) async-start(), calls=%async_computation.9 | async-start | bytes 2359296 | tf_op jit(solution)/shard_map/all_gather | solution.py:31
  103.0 130.1 %all-gather.9.cloned.1.call-start = ((), (), s32[]{:S(2)}) async-start(), calls=%async_computation.7 | async-start | bytes 2359296 | tf_op jit(solution)/shard_map/all_gather | solution.py:31
  103.7 179.2 %all-gather.17.cloned.1.call-start = ((), (), s32[]{:S(2)}) async-start(), calls=%async_computation.11 | async-start | bytes 2359296 | tf_op jit(solution)/shard_map/all_gather | solution.py:31
  134.0 51.2 %copy-start.3 = (f32[1,128,4,256]{1,3,2,0:T(8,128)S(1)}, f32[1,128,4,256]{1,3,2,0:T(8,128)}, u32[]{:S(2)}) copy-start(f32[1,128,4,256]{1,3,2,0:T(8,128)} %get-tuple-element.14) | copy-start | bytes 1572868
  181.8 3.6 copy-start.1
  185.2 147.4 %all-gather.15.cloned.1.call-start = ((), (), s32[]{:S(2)}) async-start(), calls=%async_computation.10 | async-start | bytes 2359296 | tf_op jit(solution)/shard_map/all_gather | solution.py:31
  236.2 146.6 %all-gather.19.cloned.1.call-start = ((), (), s32[]{:S(2)}) async-start(), calls=%async_computation.12 | async-start | bytes 2359296 | tf_op jit(solution)/shard_map/all_gather | solution.py:31
  257.1 4.8 %copy-start.14 = (f32[128,1024]{1,0:T(8,128)S(1)}, f32[128,1024]{1,0:T(8,128)}, u32[]{:S(2)}) copy-start(f32[128,1024]{1,0:T(8,128)} %copy.118) | copy-start | bytes 1572868
  261.9 3.2 copy-start.16
  261.9 3.2 copy-start.17
  261.9 3.2 copy-start.18
  261.9 3.2 copy-start.15
  265.1 19.9 %copy-start.12 = (bf16[128,1024]{1,0:T(8,128)(2,1)S(1)}, bf16[128,1024]{1,0:T(8,128)(2,1)}, u32[]{:S(2)}) copy-start(bf16[128,1024]{1,0:T(8,128)(2,1)} %convolution_convert_fusion.3) | copy-start | bytes 786436
  288.4 46.2 %copy-start.13 = (bf16[128,1024]{1,0:T(8,128)(2,1)S(1)}, bf16[128,1024]{1,0:T(8,128)(2,1)}, u32[]{:S(2)}) copy-start(bf16[128,1024]{1,0:T(8,128)(2,1)} %convolution_convert_fusion.4) | copy-start | bytes 786436
  334.6 48.1 %copy-start.2 = (bf16[1,128,4,256]{1,3,2,0:T(8,128)(2,1)S(1)}, bf16[1,128,4,256]{1,3,2,0:T(8,128)(2,1)}, u32[]{:S(2)}) copy-start(bf16[1,128,4,256]{1,3,2,0:T(8,128)(2,1)} %get-tuple-element.18) | copy-start | bytes 786436
  385.0 40.0 %copy-start.10 = (bf16[128,1024]{1,0:T(8,128)(2,1)S(1)}, bf16[128,1024]{1,0:T(8,128)(2,1)}, u32[]{:S(2)}) copy-start(bf16[128,1024]{1,0:T(8,128)(2,1)} %get-tuple-element.37) | copy-start | bytes 786436
  386.0 41.6 %copy-start.11 = (bf16[128,1024]{1,0:T(8,128)(2,1)S(1)}, bf16[128,1024]{1,0:T(8,128)(2,1)}, u32[]{:S(2)}) copy-start(bf16[128,1024]{1,0:T(8,128)(2,1)} %get-tuple-element.39) | copy-start | bytes 786436
  386.0 43.9 %all-to-all-start.5 = ((bf16[3,4,128,256]{3,2,0,1:T(8,128)(2,1)}), bf16[3,4,128,256]{3,2,0,1:T(8,128)(2,1)S(1)}, u32[]{:S(2)}, u32[]{:S(2)}) async-start(bf16[3,4,128,256]{3,2,0,1:T(8,128)(2,1)} %maximum_bitcast_fusion.1), calls=%async_computation.5 | async-start | bytes 1572864 | tf_op jit(solution)/shard_map/all_to_all | solution.py:27
  429.9 15.9 %all-to-all-start.3 = ((bf16[3,4,128,256]{3,2,0,1:T(8,128)(2,1)}), bf16[3,4,128,256]{3,2,0,1:T(8,128)(2,1)}, u32[]{:S(2)}, u32[]{:S(2)}) async-start(bf16[3,4,128,256]{3,2,0,1:T(8,128)(2,1)} %maximum_bitcast_fusion), calls=%async_computation.3 | async-start | bytes 1572864 | tf_op jit(solution)/shard_map/all_to_all | solution.py:27
  445.8 17.9 %all-to-all-start.6 = ((bf16[8,128,256]{2,1,0:T(8,128)(2,1)}), bf16[8,128,256]{2,1,0:T(8,128)(2,1)S(1)}, u32[]{:S(2)}, u32[]{:S(2)}) async-start(bf16[8,128,256]{2,1,0:T(8,128)(2,1)} %select_select_fusion), calls=%async_computation.6 | async-start | bytes 1048576 | tf_op jit(solution)/shard_map/all_to_all | solution.py:109
  449.3 2.0 copy-start.5
  449.3 2.0 copy-start.7
  449.3 2.0 copy-start.8
  449.3 2.0 copy-start.9
Sparse Core Ops, SparseCore 0:
  82.3 48.3 all-gather.10
  133.3 48.5 all-gather.12
  184.5 48.5 all-gather.8
  235.6 47.2 all-gather.16
  284.9 47.6 all-gather.14
  335.1 47.6 all-gather.18
where the time goes:
time: 473 us; the launch traced here: 471 us
  waiting for transfers between devices  241 us (51%)
  blocking collectives  129 us (27%)
  matrix products  32 us (7%)
  local copies, waits for them, and re-layouts  23.3 us (5%)
  other arithmetic  19.3 us (4%)
  between operations  15.3 us (3%)
  starting transfers between devices  11.5 us (2%)
    all_gather x6, waiting for transfers between devices, gather_rows(): return lax.all_gather(rows, 'dp', axis=0, tiled=True)  222 us
    all_to_all x1, blocking collectives, shards(): lax.all_to_all(partial, 'dp', split_axis=0, concat_axis=0, tiled=True)  55.4 us
    all_to_all x3, blocking collectives, to_tile(): out = lax.all_to_all(blocks, 'mp', split_axis=1, concat_axis=1, tiled=True)  42.9 us
    dot_general x10, matrix products, contract(): lax.dot_general(left, right, (((left_dim,), (right_dim,)), ((), ())), pre...  32 us
    all_gather x1, blocking collectives, shards(): everyone = lax.all_gather(packed, 'dp', axis=0, tiled=True)  30.5 us
    all_to_all x1, waiting for transfers between devices, shards(): lax.all_to_all(slots, 'dp', split_axis=0, concat_axis=0, tiled=True)  9.82 us
  transfers between devices with their start and end apart: 9, of which 8 were waited for; matrix products, arithmetic and copies ran while one was open for 13% of the time, Pallas kernels for 0%

commit v1 on v0

--- a/solution.py
+++ b/solution.py
@@ -109,7 +109,9 @@
     update_slot = lax.all_to_all(slots, "dp", split_axis=0, concat_axis=0, tiled=True)
     update_slot = update_slot.reshape(1, full, width)
     packed = jnp.concatenate([norm_grads[0], norm_m, norm_v])[None]
-    everyone = lax.all_gather(packed, "dp", axis=0, tiled=True)
+    everyone = jnp.concatenate(
+        lax.all_to_all(jnp.stack([packed] * lax.axis_size("dp")), "dp", 0, 0), axis=0
+    )
     size = norm_grads.shape[1]
     part = norm_m.shape[0]
     norm_total = jnp.sum(everyone[:, :size], axis=0)

time: 473 us -> 447 us (0.945)
  blocking collectives: 129 us -> 98.3 us
    all_gather x1 -> x0, blocking collectives: 30.5 us -> none  [shards(): everyone = lax.all_gather(packed, 'dp', axis=0, tiled=True)]
  transfers between devices with their start and end apart: 9 -> 10, of which waited for: 8 -> 8; matrix products, arithmetic and copies ran while one was open for 13% -> 14% of each run, Pallas kernels for 0% -> 0%
where the time goes in v1:
time: 447 us; the launch traced here: 445 us
  waiting for transfers between devices  241 us (54%)
  blocking collectives  98.3 us (22%)
  matrix products  32 us (7%)
  local copies, waits for them, and re-layouts  24.6 us (6%)
  other arithmetic  19.3 us (4%)
  between operations  15.3 us (3%)
  starting transfers between devices  15.1 us (3%)
    all_gather x6, waiting for transfers between devices, gather_rows(): return lax.all_gather(rows, 'dp', axis=0, tiled=True)  220 us
    all_to_all x1, blocking collectives, shards(): lax.all_to_all(partial, 'dp', split_axis=0, concat_axis=0, tiled=True)  55.4 us
    all_to_all x3, blocking collectives, to_tile(): out = lax.all_to_all(blocks, 'mp', split_axis=1, concat_axis=1, tiled=True)  42.9 us
    dot_general x10, matrix products, contract(): lax.dot_general(left, right, (((left_dim,), (right_dim,)), ((), ())), pre...  32 us
    all_to_all x2, waiting for transfers between devices, to_home(): return lax.all_to_all(out, 'mp', split_axis=1, concat_axis=1, tiled=True)  9.86 us
    all_to_all x1, waiting for transfers between devices, shards(): lax.all_to_all(slots, 'dp', split_axis=0, concat_axis=0, tiled=True)  9.82 us
    unnamed x55, local copies, waits for them, and re-layouts  9.04 us
  transfers between devices with their start and end apart: 10, of which 8 were waited for; matrix products, arithmetic and copies ran while one was open for 14% of the time, Pallas kernels for 0%

profile of v1, /device:TPU:0, one launch (start us, length us, event | category | flops | bytes accessed | tf_op | source)
XLA Modules:
  0.0 445.3 jit_solution(7328829045342619156)
XLA Ops:
  7.2 2.2 copy.123
  9.5 2.4 convolution_convert_fusion
  11.9 55.4 %all_to_all.40 = bf16[8,128,1024]{2,1,0:T(8,128)(2,1)} all-to-all(bf16[8,128,1024]{2,1,0:T(8,128)(2,1)S(1)} %bitcast.132), channel_id=1, replica_groups=mesh['dp'=8,'mp'=4] {'dp'}, dimensions={0} | all-to-all | bytes 4194304 | tf_op jit(solution)/shard_map/all_to_all | solution.py:63
  67.3 2.0 reduce_sum.41
  70.2 1.1 copy.98
  71.3 9.1 %all_to_all.41 = bf16[1,4,128,256]{3,2,0,1:T(8,128)(2,1)} all-to-all(bf16[1,4,128,256]{3,2,0,1:T(8,128)(2,1)S(1)} %copy.98), channel_id=1, replica_groups=mesh['dp'=8,'mp'=4] {'mp'}, dimensions={1} | all-to-all | bytes 524288 | tf_op jit(solution)/shard_map/all_to_all | solution.py:19
  80.4 1.8 copy.99
  82.6 1.2 copy.93
  83.8 1.2 copy.92
  85.2 16.9 %all_to_all.42 = bf16[4,4,128,256]{2,3,0,1:T(8,128)(2,1)S(1)} all-to-all(bf16[4,4,128,256]{2,3,0,1:T(8,128)(2,1)S(1)} %pad_maximum_fusion), channel_id=1, replica_groups=mesh['dp'=8,'mp'=4] {'mp'}, dimensions={1} | all-to-all | bytes 2097152 | tf_op jit(solution)/shard_map/all_to_all | solution.py:19
  103.8 1.1 convert_multiply_fusion.5
  104.8 1.2 copy.117
  106.1 24.6 %all-gather.9.cloned.1.call-done = bf16[1024,1024]{0,1:T(8,128)(2,1)} async-done(((bf16[128,1024]{0,1:T(8,128)(2,1)}), bf16[1024,1024]{0,1:T(8,128)(2,1)}) %all-gather.9.cloned.1.call-update) | async-done | bytes 2097168 | tf_op jit(solution)/shard_map/all_gather | solution.py:31
  130.7 3.4 fusion.89
  134.1 47.8 %all-gather.11.cloned.1.call-done = bf16[1024,1024]{0,1:T(8,128)(2,1)} async-done(((bf16[128,1024]{0,1:T(8,128)(2,1)}), bf16[1024,1024]{0,1:T(8,128)(2,1)}) %all-gather.11.cloned.1.call-update) | async-done | bytes 2097168 | tf_op jit(solution)/shard_map/all_gather | solution.py:31
  181.8 3.3 convolution_convert_fusion.3
  185.5 2.8 fusion.90
  188.2 44.8 %all-gather.7.cloned.1.call-done = bf16[1024,1024]{0,1:T(8,128)(2,1)} async-done(((bf16[128,1024]{0,1:T(8,128)(2,1)}), bf16[1024,1024]{0,1:T(8,128)(2,1)}) %all-gather.7.cloned.1.call-update) | async-done | bytes 2097168 | tf_op jit(solution)/shard_map/all_gather | solution.py:31
  233.0 3.1 convolution_convert_fusion.4
  236.2 1.2 copy.108
  237.4 1.2 copy.109
  238.8 17.0 %all_to_all.43 = f32[2,4,128,256]{2,3,0,1:T(8,128)S(1)} all-to-all(f32[2,4,128,256]{2,3,0,1:T(8,128)S(1)} %pad_maximum_fusion.1), channel_id=1, replica_groups=mesh['dp'=8,'mp'=4] {'mp'}, dimensions={1} | all-to-all | bytes 2097152 | tf_op jit(solution)/shard_map/all_to_all | solution.py:19
  257.1 4.8 %fusion.91 = (bf16[128,1024]{1,0:T(8,128)(2,1)}, f32[128,1024]{1,0:T(8,128)}) fusion(bf16[1024,1024]{0,1:T(8,128)(2,1)} %all-gather.11.cloned.1.call-done, bf16[1024,1024]{0,1:T(8,128)(2,1)} %all-gather.9.cloned.1.call-done, bf16[1024,1024]{0,1:T(8,128)(2,1)} %all-gather.7.cloned.1.call-done, s32[]{:T(128)S(6)} %select_n.36), kind=kOutput, calls=%fused_computation.119 | convolution fusion | flops 537133056 | bytes 5242884 | tf_op jit(solution)/shard_map/dot_general | solution.py:13
  261.9 3.1 convolution_convert_fusion.2
  265.8 3.5 all-to-all-start.7
  269.4 13.6 %all-gather.15.cloned.1.call-done = bf16[1024,1024]{1,0:T(8,128)(2,1)} async-done(((bf16[128,1024]{1,0:T(8,128)(2,1)}), bf16[1024,1024]{1,0:T(8,128)(2,1)}) %all-gather.15.cloned.1.call-update) | async-done | bytes 2097168 | tf_op jit(solution)/shard_map/all_gather | solution.py:31
  282.9 2.1 fusion.2
  285.0 48.4 %all-gather.13.cloned.1.call-done = bf16[1024,1024]{1,0:T(8,128)(2,1)} async-done(((bf16[128,1024]{1,0:T(8,128)(2,1)}), bf16[1024,1024]{1,0:T(8,128)(2,1)}) %all-gather.13.cloned.1.call-update) | async-done | bytes 2097168 | tf_op jit(solution)/shard_map/all_gather | solution.py:31
  333.4 2.1 fusion
  335.5 3.5 fusion.24
  339.0 3.5 fusion.27
  342.5 41.1 %all-gather.17.cloned.1.call-done = bf16[1024,1024]{1,0:T(8,128)(2,1)} async-done(((bf16[128,1024]{1,0:T(8,128)(2,1)}), bf16[1024,1024]{1,0:T(8,128)(2,1)}) %all-gather.17.cloned.1.call-update) | async-done | bytes 2097168 | tf_op jit(solution)/shard_map/all_gather | solution.py:31
  383.6 2.1 convolution_convert_fusion.1
  387.3 3.6 all-to-all-start.5
  392.2 1.3 iota_compare_fusion
  393.5 1.3 iota_compare_fusion.2
  395.5 1.8 stack.61
  397.4 1.7 copy.100
  399.9 1.7 copy.102
  401.8 2.0 maximum_bitcast_fusion
  403.8 4.2 all-to-all-start.3
  408.8 1.1 select_select_fusion
  409.9 9.9 %all-to-all-done.3 = bf16[3,4,128,256]{3,2,0,1:T(8,128)(2,1)} async-done(((bf16[3,4,128,256]{3,2,0,1:T(8,128)(2,1)}), bf16[3,4,128,256]{3,2,0,1:T(8,128)(2,1)}, u32[]{:S(2)}, u32[]{:S(2)}) %all-to-all-start.3) | async-done | bytes 786464 | tf_op jit(solution)/shard_map/all_to_all | solution.py:27
  419.7 3.5 all-to-all-start.6
  423.9 1.3 convert_element_type.101
  425.3 1.5 fusion.48
  426.7 1.1 fusion.54
  427.8 9.8 %all-to-all-done.6 = bf16[8,128,256]{2,1,0:T(8,128)(2,1)S(1)} async-done(((bf16[8,128,256]{2,1,0:T(8,128)(2,1)}), bf16[8,128,256]{2,1,0:T(8,128)(2,1)S(1)}, u32[]{:S(2)}, u32[]{:S(2)}) %all-to-all-start.6) | async-done | bytes 524320 | tf_op jit(solution)/shard_map/all_to_all | solution.py:109
  (94 shorter events, 11.8 us)
Async XLA Ops:
  7.2 2.3 copy-start
  7.2 123.5 %all-gather.9.cloned.1.call-start = ((), (), s32[]{:S(2)}) async-start(), calls=%async_computation.9 | async-start | bytes 2359296 | tf_op jit(solution)/shard_map/all_gather | solution.py:31
  67.3 14.9 %copy-start.4 = (f32[4,128,256]{2,1,0:T(8,128)S(1)}, f32[4,128,256]{2,1,0:T(8,128)}, u32[]{:S(2)}) copy-start(f32[4,128,256]{2,1,0:T(8,128)} %param.19) | copy-start | bytes 1572868
  69.3 13.1 %copy-start.6 = (f32[4,128,256]{2,1,0:T(8,128)S(1)}, f32[4,128,256]{2,1,0:T(8,128)}, u32[]{:S(2)}) copy-start(f32[4,128,256]{2,1,0:T(8,128)} %param.18) | copy-start | bytes 1572868
  82.2 99.7 %all-gather.11.cloned.1.call-start = ((), (), s32[]{:S(2)}) async-start(), calls=%async_computation.10 | async-start | bytes 2359296 | tf_op jit(solution)/shard_map/all_gather | solution.py:31
  103.0 130.1 %all-gather.7.cloned.1.call-start = ((), (), s32[]{:S(2)}) async-start(), calls=%async_computation.8 | async-start | bytes 2359296 | tf_op jit(solution)/shard_map/all_gather | solution.py:31
  103.7 179.2 %all-gather.15.cloned.1.call-start = ((), (), s32[]{:S(2)}) async-start(), calls=%async_computation.12 | async-start | bytes 2359296 | tf_op jit(solution)/shard_map/all_gather | solution.py:31
  134.0 51.2 %copy-start.3 = (f32[1,128,4,256]{1,3,2,0:T(8,128)S(1)}, f32[1,128,4,256]{1,3,2,0:T(8,128)}, u32[]{:S(2)}) copy-start(f32[1,128,4,256]{1,3,2,0:T(8,128)} %get-tuple-element.14) | copy-start | bytes 1572868
  181.8 3.6 copy-start.1
  185.2 148.2 %all-gather.13.cloned.1.call-start = ((), (), s32[]{:S(2)}) async-start(), calls=%async_computation.11 | async-start | bytes 2359296 | tf_op jit(solution)/shard_map/all_gather | solution.py:31
  236.2 147.4 %all-gather.17.cloned.1.call-start = ((), (), s32[]{:S(2)}) async-start(), calls=%async_computation.13 | async-start | bytes 2359296 | tf_op jit(solution)/shard_map/all_gather | solution.py:31
  257.1 4.8 %copy-start.14 = (f32[128,1024]{1,0:T(8,128)S(1)}, f32[128,1024]{1,0:T(8,128)}, u32[]{:S(2)}) copy-start(f32[128,1024]{1,0:T(8,128)} %copy.118) | copy-start | bytes 1572868
  261.9 3.2 copy-start.18
  261.9 3.2 copy-start.19
  261.9 3.2 copy-start.20
  265.8 121.5 %all-to-all-start.7 = ((f32[8,1,2560]{2,1,0:T(1,128)}), f32[8,1,2560]{2,1,0:T(1,128)S(1)}, u32[]{:S(2)}, u32[]{:S(2)}) async-start(f32[8,1,2560]{2,1,0:T(1,128)} %stack.72), calls=%async_computation.7 | async-start | bytes 163840 | tf_op jit(solution)/shard_map/all_to_all | solution.py:113
  269.3 66.1 %copy-start.12 = (bf16[128,1024]{1,0:T(8,128)(2,1)S(1)}, bf16[128,1024]{1,0:T(8,128)(2,1)}, u32[]{:S(2)}) copy-start(bf16[128,1024]{1,0:T(8,128)(2,1)} %convolution_convert_fusion.3) | copy-start | bytes 786436
  335.5 3.5 copy-start.13
  339.0 44.6 %copy-start.2 = (bf16[1,128,4,256]{1,3,2,0:T(8,128)(2,1)S(1)}, bf16[1,128,4,256]{1,3,2,0:T(8,128)(2,1)}, u32[]{:S(2)}) copy-start(bf16[1,128,4,256]{1,3,2,0:T(8,128)(2,1)} %get-tuple-element.18) | copy-start | bytes 786436
  386.1 4.9 %copy-start.17 = (s32[5]{0:T(128)S(1)}, s32[5]{0:T(128)}, u32[]{:S(2)}) copy-start(s32[5]{0:T(128)} %param.15) | copy-start | bytes 64
  386.3 12.7 %copy-start.10 = (bf16[128,1024]{1,0:T(8,128)(2,1)S(1)}, bf16[128,1024]{1,0:T(8,128)(2,1)}, u32[]{:S(2)}) copy-start(bf16[128,1024]{1,0:T(8,128)(2,1)} %get-tuple-element.37) | copy-start | bytes 786436
  387.3 14.3 %copy-start.11 = (bf16[128,1024]{1,0:T(8,128)(2,1)S(1)}, bf16[128,1024]{1,0:T(8,128)(2,1)}, u32[]{:S(2)}) copy-start(bf16[128,1024]{1,0:T(8,128)(2,1)} %get-tuple-element.39) | copy-start | bytes 786436
  387.3 16.5 %all-to-all-start.5 = ((bf16[3,4,128,256]{3,2,0,1:T(8,128)(2,1)}), bf16[3,4,128,256]{3,2,0,1:T(8,128)(2,1)S(1)}, u32[]{:S(2)}, u32[]{:S(2)}) async-start(bf16[3,4,128,256]{3,2,0,1:T(8,128)(2,1)} %maximum_bitcast_fusion.1), calls=%async_computation.5 | async-start | bytes 1572864 | tf_op jit(solution)/shard_map/all_to_all | solution.py:27
  394.9 0.6 copy-start.15
  401.6 6.4 %copy-start.16 = (f32[8,1,2560]{2,0,1:T(8,128)S(1)}, f32[8,1,2560]{2,0,1:T(8,128)}, u32[]{:S(2)}) copy-start(f32[8,1,2560]{2,0,1:T(8,128)} %copy-done.15) | copy-start | bytes 245764
  403.8 15.9 %all-to-all-start.3 = ((bf16[3,4,128,256]{3,2,0,1:T(8,128)(2,1)}), bf16[3,4,128,256]{3,2,0,1:T(8,128)(2,1)}, u32[]{:S(2)}, u32[]{:S(2)}) async-start(bf16[3,4,128,256]{3,2,0,1:T(8,128)(2,1)} %maximum_bitcast_fusion), calls=%async_computation.3 | async-start | bytes 1572864 | tf_op jit(solution)/shard_map/all_to_all | solution.py:27
  419.7 17.9 %all-to-all-start.6 = ((bf16[8,128,256]{2,1,0:T(8,128)(2,1)}), bf16[8,128,256]{2,1,0:T(8,128)(2,1)S(1)}, u32[]{:S(2)}, u32[]{:S(2)}) async-start(bf16[8,128,256]{2,1,0:T(8,128)(2,1)} %select_select_fusion), calls=%async_computation.6 | async-start | bytes 1048576 | tf_op jit(solution)/shard_map/all_to_all | solution.py:109
  423.2 2.0 copy-start.5
  423.2 2.0 copy-start.7
  423.2 2.0 copy-start.8
  423.3 2.0 copy-start.9
Sparse Core Ops, SparseCore 0:
  82.3 48.3 all-gather.8
  133.3 48.5 all-gather.10
  184.5 48.5 all-gather.6
  235.6 47.2 all-gather.14
  284.9 48.4 all-gather.12
  335.9 47.6 all-gather.16
